TPU v7x, 32 devices: a whole 2x2x4 slice. The times are simulated.
32 devices in a mesh: aa: 4 (over y, x), ta: 8 (over z, core).
Axes of the slice: x: 2, y: 2, z: 4, core: 2. Of those that a mesh axis runs over, the one named last changes fastest.
Arguments:
- voltages: bfloat16 [1024, 49152], P('aa', 'ta'), may hold values from -6 to 6
Outputs:
- visibility: bfloat16 [2, 512, 1024, 1024], P(None, 'aa', 'ta')
All inputs are finite; a program needn't handle non-finite values.
Results may differ from a plain program's by a relative error of at most 0.0078.
Values may be sent and summed in bfloat16 or wider, within the bound.
A program may use at most 256 MiB of HBM per device.

v0:
```python
import jax
import jax.numpy as jnp
from jax import lax
from jax.sharding import PartitionSpec as P

INPUTS = 1024
FRAME = 2048
CHANNELS = 512
TAPS = 4


def shifted(value, axis, steps):
    count = lax.axis_size(axis)
    leading, last = (max(0, -steps), min(count, count - steps))
    return lax.ppermute(value, axis, [(source, source + steps) for source in range(leading, last)])


def make_window():
    length = TAPS * FRAME
    place = jnp.arange(length, dtype=jnp.float32)
    spread = (place - length / 2 + 0.5) / FRAME
    taper = 0.5 - 0.5 * jnp.cos(2.0 * jnp.pi * (place + 0.5) / length)
    return (jnp.sinc(spread) * taper).reshape(TAPS, FRAME)


def make_table():
    sample = jnp.arange(FRAME, dtype=jnp.int32)[:, None]
    column = jnp.arange(2 * CHANNELS, dtype=jnp.int32)[None, :]
    channel = column % CHANNELS
    phase = (sample * channel % FRAME).astype(jnp.float32) * (2.0 * jnp.pi / FRAME)
    norm = 1.0 / jnp.sqrt(jnp.float32(FRAME))
    values = jnp.where(column < CHANNELS, jnp.cos(phase), -jnp.sin(phase))
    return (values * norm).astype(jnp.bfloat16)


def left_operand(rows):
    first = jnp.concatenate([rows[0], rows[1]], axis=2)
    second = jnp.concatenate([rows[1], -rows[0]], axis=2)
    return jnp.stack([first, second], axis=0)


def correlate(left, columns):
    return jnp.einsum("pcsi,pcsj->cij", left, columns, preferred_element_type=jnp.float32)


def finish(merged, row_count, scale):
    chan_dev = merged.shape[0]
    shaped = merged.reshape(chan_dev, 2, row_count, merged.shape[2])
    return (jnp.swapaxes(shaped, 0, 1) * scale).astype(jnp.bfloat16)


def per_device(voltages):
    in_dev = voltages.shape[0]
    spec_dev = voltages.shape[1] // FRAME
    n_ta = lax.axis_size("ta")
    frames = voltages.reshape(in_dev, spec_dev, FRAME)
    earlier = shifted(frames, "ta", 1)
    padded = jnp.concatenate([earlier, frames], axis=1)
    window = make_window()
    filtered = jnp.zeros((in_dev, spec_dev, FRAME), jnp.float32)
    for k in range(TAPS):
        filtered = filtered + window[k] * padded[:, k : k + spec_dev, :].astype(jnp.float32)
    filtered = filtered.astype(jnp.bfloat16)
    table = make_table()
    spectra = jnp.einsum("isn,nk->ksi", filtered, table, preferred_element_type=jnp.float32).astype(
        jnp.bfloat16
    )
    spectra = spectra.reshape(2, CHANNELS, spec_dev, in_dev)
    row_count = INPUTS // n_ta
    scale = 1.0 / (spec_dev * n_ta)
    own_rows = lax.all_to_all(
        lax.all_to_all(spectra, "aa", split_axis=1, concat_axis=3, tiled=True),
        "ta",
        split_axis=3,
        concat_axis=2,
        tiled=True,
    )
    left = left_operand(own_rows)
    merged = correlate(left, lax.all_gather(own_rows, "ta", axis=3, tiled=True))
    return finish(merged, row_count, scale)


def solution(mesh):
    in_specs = (P("aa", "ta"),)
    out_specs = P(None, "aa", "ta", None)
    return jax.shard_map(
        per_device, mesh=mesh, in_specs=in_specs, out_specs=out_specs, check_vma=False
    )
```

profile of v0, /device:TPU:1, one launch (start us, length us, event | category | flops | bytes accessed | tf_op | source)
XLA Modules:
  0.0 357.5 jit_solution(15409674039536836981)
XLA Ops:
  6.5 0.0 all-gather.2.cloned.1.call-start
  6.5 3.2 copy.47
  9.7 4.6 %collective-permute-start = (bf16[256,3,2048]{0,2,1:T(8,128)(2,1)S(1)}, bf16[256,3,2048]{0,2,1:T(8,128)(2,1)S(1)}, u32[]{:S(2)}, u32[]{:S(2)}) collective-permute-start(bf16[256,3,2048]{0,2,1:T(8,128)(2,1)S(1)} %bitcast.41), channel_id=1, source_target_pairs={{0,1},{1,2},{2,3},{3,4},{4,5},{5,6},{6,7},{8,9},{9,10},{10,11},{11... | collective-permute-start | bytes 9437192 | tf_op jit(solution)/shard_map/ppermute | solution.py:15
  14.3 0.2 fusion.34
  14.5 34.0 %collective-permute-done = bf16[256,3,2048]{0,2,1:T(8,128)(2,1)S(1)} collective-permute-done((bf16[256,3,2048]{0,2,1:T(8,128)(2,1)S(1)}, bf16[256,3,2048]{0,2,1:T(8,128)(2,1)S(1)}, u32[]{:S(2)}, u32[]{:S(2)}) %collective-permute-start) | collective-permute-done | bytes 3145760 | tf_op jit(solution)/shard_map/ppermute | solution.py:15
  48.5 3.1 add_convert_fusion.7
  51.6 37.5 %fusion.27 = bf16[1024,256,3]{1,0,2:T(8,128)(2,1)S(1)} fusion(s32[1024]{0:T(1024)S(1)} %add_select_fusion.1, pred[1024]{0:T(1024)(128)(4,1)S(1)} %iota_compare_fusion, bf16[256,3,2048]{0,2,1:T(8,128)(2,1)S(1)} %add_convert_fusion.7), kind=kOutput, calls=%fused_computation.35 | convolution fusion | flops 3259760640 | bytes 4723712 | tf_op jit(solution)/shard_map/isn,nk->ksi/dot_general | solution.py:65
  89.1 1.6 copy.49
  90.7 14.8 %all_to_all.36 = bf16[2,512,3,256]{3,0,2,1:T(2,128)(2,1)S(1)} all-to-all(bf16[2,512,3,256]{3,0,2,1:T(2,128)(2,1)S(1)} %copy.49), channel_id=1, replica_groups=mesh['aa'=4,'ta'=8] {'aa'}, dimensions={1} | all-to-all | bytes 3145728 | tf_op jit(solution)/shard_map/all_to_all | solution.py:72
  105.5 0.2 copy.50
  105.8 0.9 copy.51
  106.7 1.6 copy.52
  108.3 49.6 %all_to_all.37 = bf16[2,128,3,1024]{1,0,2,3:T(2,128)(2,1)S(1)} all-to-all(bf16[2,128,3,1024]{1,0,2,3:T(2,128)(2,1)S(1)} %copy.52), channel_id=1, replica_groups=mesh['aa'=4,'ta'=8] {'ta'}, dimensions={3} | all-to-all | bytes 3145728 | tf_op jit(solution)/shard_map/all_to_all | solution.py:71
  157.9 0.2 copy.53
  158.1 0.9 copy.60
  159.0 2.2 copy.61
  161.2 0.0 all-gather.2.cloned.1.call-update
  161.2 0.2 fusion.69
  161.3 0.4 copy.55
  161.7 0.5 copy.57
  162.3 0.4 copy.54
  162.6 0.6 fusion.70
  163.3 1.5 maximum_bitcast_fusion
  164.7 111.9 %all-gather.2.cloned.1.call-done = bf16[2,128,24,1024]{3,2,0,1:T(8,128)(2,1)} async-done(((bf16[2,128,24,128]{3,2,0,1:T(8,128)(2,1)}), bf16[2,128,24,1024]{3,2,0,1:T(8,128)(2,1)}) %all-gather.2.cloned.1.call-update) | async-done | bytes 12582928 | tf_op jit(solution)/shard_map/all_gather | solution.py:79
  276.7 29.8 %fusion = bf16[128,256,1024]{2,1,0:T(8,128)(2,1)} fusion(bf16[2,128,24,1024]{3,2,0,1:T(8,128)(2,1)} %all-gather.2.cloned.1.call-done, bf16[1,128,24,256]{3,2,0,1:T(8,128)(2,1)} %get-tuple-element.8, bf16[1,128,24,256]{3,2,0,1:T(8,128)(2,1)S(1)} %get-tuple-element.7), kind=kOutput, calls=%fused_computation.1 | convolution fusion | flops 3289907200 | bytes 82837504 | tf_op jit(solution)/shard_map/pcsi,pcsj->cij/dot_general | solution.py:43
  306.5 44.1 %copy.68 = bf16[128,2,128,1024]{3,2,0,1:T(8,128)(2,1)} copy(bf16[128,2,128,1024]{3,2,1,0:T(8,128)(2,1)} %bitcast.17) | data formatting | bytes 134217728 | tf_op jit(solution)/shard_map/convert_element_type | solution.py:49
  (3 shorter events, 0.0 us)
Async XLA Ops:
  6.5 270.1 %all-gather.2.cloned.1.call-start = ((), (), s32[]{:S(2)}) async-start(), calls=%async_computation.2 | async-start | bytes 14155776 | tf_op jit(solution)/shard_map/all_gather | solution.py:79
  9.7 38.8 %collective-permute-start = (bf16[256,3,2048]{0,2,1:T(8,128)(2,1)S(1)}, bf16[256,3,2048]{0,2,1:T(8,128)(2,1)S(1)}, u32[]{:S(2)}, u32[]{:S(2)}) collective-permute-start(bf16[256,3,2048]{0,2,1:T(8,128)(2,1)S(1)} %bitcast.41), channel_id=1, source_target_pairs={{0,1},{1,2},{2,3},{3,4},{4,5},{5,6},{6,7},{8,9},{9,10},{10,11},{11... | collective-permute-start | bytes 9437192 | tf_op jit(solution)/shard_map/ppermute | solution.py:15
Sparse Core Ops, SparseCore 0:
  161.3 115.3 all-gather.1
where the time goes:
time: 358 us; the launch traced here: 357 us
  waiting for transfers between devices  146 us (41%)
  matrix products  67.3 us (19%)
  blocking collectives  64.4 us (18%)
  local copies, waits for them, and re-layouts  56.4 us (16%)
  between operations  13.5 us (4%)
  other arithmetic  5.33 us (1%)
  starting transfers between devices  4.6 us (1%)
    all_gather x1, waiting for transfers between devices, per_device(): merged = correlate(left, lax.all_gather(own_rows, 'ta', axis=3, tiled=True))  112 us
    all_to_all x1, blocking collectives, per_device(): lax.all_to_all(lax.all_to_all(spectra, 'aa', split_axis=1, concat_axis=3,...  49.6 us
    convert_element_type x1, local copies, waits for them, and re-layouts, finish(): return (jnp.swapaxes(shaped, 0, 1) * scale).astype(jnp.bfloat16)  44.1 us
    dot_general x1, matrix products, per_device(): jnp.einsum('isn,nk->ksi', filtered, table, preferred_element_type=jnp.flo...  37.5 us
    ppermute x1, waiting for transfers between devices, shifted(): lax.ppermute(value, axis, [(source, source + steps) for source in range(l...  34 us
    dot_general x1, matrix products, correlate(): jnp.einsum('pcsi,pcsj->cij', left, columns, preferred_element_type=jnp.fl...  29.8 us
    all_to_all x1, blocking collectives, per_device(): lax.all_to_all(spectra, 'aa', split_axis=1, concat_axis=3, tiled=True)  14.8 us
  transfers between devices with their start and end apart: 2, of which 2 were waited for; matrix products, arithmetic and copies ran while one was open for 1% of the time, Pallas kernels for 0%

commit v1 on v0

--- a/solution.py
+++ b/solution.py
@@ -1,12 +1,225 @@
+import functools
+
 import jax
 import jax.numpy as jnp
+import numpy as np
 from jax import lax
+from jax.experimental import pallas as pl
+from jax.experimental.pallas import tpu as pltpu
 from jax.sharding import PartitionSpec as P
 
 INPUTS = 1024
 FRAME = 2048
 CHANNELS = 512
 TAPS = 4
+LANES = 128
+
+
+def make_window():
+    length = TAPS * FRAME
+    place = np.arange(length, dtype=np.float64)
+    spread = (place - length / 2 + 0.5) / FRAME
+    taper = 0.5 - 0.5 * np.cos(2.0 * np.pi * (place + 0.5) / length)
+    return (np.sinc(spread) * taper).reshape(TAPS, FRAME).astype(np.float32)
+
+
+def make_turns():
+    channel = np.arange(CHANNELS)[:, None]
+
+    def turn(step, count):
+        phase = (channel * np.arange(count)[None, :] * step % FRAME) * (2.0 * np.pi / FRAME)
+        return np.cos(phase), np.sin(phase)
+
+    coarse_cos, coarse_sin = turn(LANES, FRAME // LANES)
+    fine_cos, fine_sin = turn(1, LANES)
+    norm = 1.0 / np.sqrt(FRAME)
+    coarse = np.concatenate([coarse_cos, coarse_sin], axis=1)
+    fine = np.concatenate([fine_cos * norm, fine_sin * norm], axis=1)
+    return coarse.astype(np.float32), fine.astype(np.float32)
+
+
+def table_kernel(coarse_ref, fine_ref, out_ref):
+    count = FRAME // LANES
+
+    @pl.loop(0, CHANNELS // 16)
+    def _(step):
+        at = pl.multiple_of(step * 16, 16)
+        here = pl.ds(at, 16)
+        fine_cos, fine_sin = fine_ref[here, :LANES], fine_ref[here, LANES:]
+        for a in range(count):
+            columns = slice(a * LANES, (a + 1) * LANES)
+            coarse_cos = coarse_ref[here, a : a + 1]
+            coarse_sin = coarse_ref[here, count + a : count + a + 1]
+            real = coarse_cos * fine_cos - coarse_sin * fine_sin
+            imag = -(coarse_sin * fine_cos + coarse_cos * fine_sin)
+            out_ref[0, here, columns] = real.astype(jnp.bfloat16)
+            out_ref[1, here, columns] = imag.astype(jnp.bfloat16)
+
+
+def make_table():
+    coarse, fine = make_turns()
+    return pl.pallas_call(
+        table_kernel,
+        out_shape=jax.ShapeDtypeStruct((2, CHANNELS, FRAME), jnp.bfloat16),
+        compiler_params=pltpu.CompilerParams(vmem_limit_bytes=16 * 2**20),
+        cost_estimate=pl.CostEstimate(
+            flops=2**23, bytes_accessed=2**23, transcendentals=0
+        ),
+    )(jnp.asarray(coarse), jnp.asarray(fine))
+
+
+def dft_kernel(core_ref, *refs, pick, count, unread):
+    window_ref, table_ref = refs[-4 - unread : -2 - unread]
+    blocks, (out_ref, filtered_ref) = refs[: -4 - unread], refs[-2:]
+    inputs = blocks[0].shape[0]
+    rows = min(16, inputs)
+
+    def filter_from(earlier, current):
+        def frame(at, index):
+            ref, place = (earlier, index) if index < count else (current, index - count)
+            return ref[pl.ds(at, rows), place * FRAME : (place + 1) * FRAME].astype(jnp.float32)
+
+        @pl.loop(0, inputs // rows)
+        def _(step):
+            at = pl.multiple_of(step * rows, rows)
+            for s in range(count):
+                total = window_ref[0:1, :] * frame(at, s + count - TAPS + 1)
+                for k in range(1, TAPS):
+                    total = total + window_ref[k : k + 1, :] * frame(at, s + k + count - TAPS + 1)
+                filtered_ref[s, pl.ds(at, rows), :] = total.astype(jnp.bfloat16)
+
+    @pl.when((pl.program_id(0) == 0) & (pl.program_id(1) == 0))
+    def _():
+        for core, (earlier, current) in enumerate(pick):
+            pl.when(core_ref[0] == core)(
+                functools.partial(filter_from, blocks[earlier], blocks[current])
+            )
+
+    for s in range(count):
+        out_ref[0, 0, s] = lax.dot_general(
+            table_ref[0],
+            filtered_ref[s],
+            (((1,), (1,)), ((), ())),
+            preferred_element_type=jnp.float32,
+        ).astype(jnp.bfloat16)
+
+
+def dft(core, blocks, pick, window, table, n_aa, count, after=()):
+    inputs = blocks[0].shape[0]
+    chan_dev = CHANNELS // n_aa
+    whole = lambda q, p, core_ref: (0, 0)
+    flops = 2 * count * inputs * FRAME * 2 * CHANNELS
+    return pl.pallas_call(
+        functools.partial(dft_kernel, pick=pick, count=count, unread=len(after)),
+        grid_spec=pltpu.PrefetchScalarGridSpec(
+            num_scalar_prefetch=1,
+            grid=(n_aa, 2),
+            in_specs=[pl.BlockSpec(block.shape, whole) for block in blocks]
+            + [
+                pl.BlockSpec((TAPS, FRAME), whole),
+                pl.BlockSpec((1, chan_dev, FRAME), lambda q, p, core_ref: (p, q, 0)),
+            ]
+            + [pl.BlockSpec(memory_space=pl.ANY)] * len(after),
+            out_specs=pl.BlockSpec(
+                (1, 1, count, chan_dev, inputs), lambda q, p, core_ref: (q, p, 0, 0, 0)
+            ),
+            scratch_shapes=[pltpu.VMEM((count, inputs, FRAME), jnp.bfloat16)],
+        ),
+        out_shape=jax.ShapeDtypeStruct((n_aa, 2, count, chan_dev, inputs), jnp.bfloat16),
+        compiler_params=pltpu.CompilerParams(vmem_limit_bytes=40 * 2**20),
+        cost_estimate=pl.CostEstimate(
+            flops=flops, bytes_accessed=len(blocks) * blocks[0].size * 2 + 2**22, transcendentals=0
+        ),
+    )(core, *blocks, window, table, *after)
+
+
+def correlate_kernel(core_ref, first_ref, second_ref, spread_ref, *refs, scale, groups):
+    out_ref, columns_ref = refs[-2:]
+    halves, chans, depth, lanes = first_ref.shape
+    full = halves * depth
+    size = columns_ref.shape[0]
+    if full < size:
+        columns_ref[full:, :] = jnp.zeros((size - full, 2 * lanes), jnp.bfloat16)
+    own = pl.ds(pl.multiple_of(core_ref[0] * lanes, lanes), lanes)
+    group_of = lax.rem(lax.broadcasted_iota(jnp.int32, (1, size), 1), depth) // (depth // groups)
+    masks = [
+        jnp.where(group_of == group, 1.0, 0.0).astype(jnp.bfloat16) for group in range(groups)
+    ]
+
+    @pl.loop(0, chans)
+    def _(c):
+        for at, ref in enumerate((first_ref, second_ref)):
+            for block in range(halves // 2):
+                place = (at * (halves // 2) + block) * depth
+                for core in range(2):
+                    columns_ref[place : place + depth, core * lanes : (core + 1) * lanes] = ref[
+                        2 * block + core, c
+                    ]
+        columns = columns_ref[...]
+        left = lax.dot_general(
+            columns_ref[:, own],
+            spread_ref[...],
+            (((0,), (0,)), ((), ())),
+            preferred_element_type=jnp.float32,
+        ).astype(jnp.bfloat16)
+        for p in range(2):
+            part = left[:, p * size : (p + 1) * size]
+            for group in range(groups):
+                total = jnp.dot(
+                    part * masks[group], columns, preferred_element_type=jnp.float32
+                )
+                out_ref[p, c, :, group * 2 * lanes : (group + 1) * 2 * lanes] = (
+                    total * scale
+                ).astype(jnp.bfloat16)
+
+
+def spread_rows(group, halves, depth, groups):
+    part = depth // groups
+    full, size = halves * depth, 256
+    row = lax.broadcasted_iota(jnp.int32, (size, 2 * size), 0)
+    column = lax.broadcasted_iota(jnp.int32, (size, 2 * size), 1)
+    turned, column = column // size, column % size
+    same = (row // depth == column // depth) & (row < full) & (column < full)
+    same = same & (row % depth // part == group)
+    row, column = row % part, column % part
+    count = part // 2
+    straight = jnp.where(row == column, 1.0, 0.0)
+    swap = jnp.where(row == column + count, 1.0, 0.0) - jnp.where(row + count == column, 1.0, 0.0)
+    values = jnp.where(turned == 1, swap, straight)
+    return jnp.where(same, values, 0.0).astype(jnp.bfloat16)
+
+
+def correlate(core, first, second, spread, result, at, chan_dev, n_aa, scale):
+    halves, chans, depth, lanes = second.shape
+    step = min(8, chans)
+    start = at // step
+    out_shape = jax.ShapeDtypeStruct((2, chan_dev, lanes, INPUTS), jnp.bfloat16)
+    extra = [] if result is None else [result]
+    return pl.pallas_call(
+        functools.partial(correlate_kernel, scale=scale, groups=n_aa),
+        grid_spec=pltpu.PrefetchScalarGridSpec(
+            num_scalar_prefetch=1,
+            grid=(chans // step,),
+            in_specs=[
+                pl.BlockSpec((halves, step, depth, lanes), lambda c, core_ref: (0, start + c, 0, 0)),
+                pl.BlockSpec((halves, step, depth, lanes), lambda c, core_ref: (0, c, 0, 0)),
+                pl.BlockSpec(spread.shape, lambda c, core_ref: (0, 0)),
+            ]
+            + [pl.BlockSpec(memory_space=pl.ANY)] * len(extra),
+            out_specs=pl.BlockSpec(
+                (2, step, lanes, INPUTS), lambda c, core_ref: (0, start + c, 0, 0)
+            ),
+            scratch_shapes=[pltpu.VMEM((256, 2 * lanes), jnp.bfloat16)],
+        ),
+        out_shape=out_shape,
+        input_output_aliases={4: 0} if extra else {},
+        compiler_params=pltpu.CompilerParams(vmem_limit_bytes=60 * 2**20),
+        cost_estimate=pl.CostEstimate(
+            flops=4 * chans * lanes * INPUTS * 256,
+            bytes_accessed=chans * (4 * lanes * INPUTS + 4 * halves * depth * lanes),
+            transcendentals=0,
+        ),
+    )(core, first, second, spread, *extra)
 
 
 def shifted(value, axis, steps):
@@ -15,7 +228,7 @@
     return lax.ppermute(value, axis, [(source, source + steps) for source in range(leading, last)])
 
 
-def make_window():
+def plain_window():
     length = TAPS * FRAME
     place = jnp.arange(length, dtype=jnp.float32)
     spread = (place - length / 2 + 0.5) / FRAME
@@ -23,7 +236,7 @@
     return (jnp.sinc(spread) * taper).reshape(TAPS, FRAME)
 
 
-def make_table():
+def plain_table():
     sample = jnp.arange(FRAME, dtype=jnp.int32)[:, None]
     column = jnp.arange(2 * CHANNELS, dtype=jnp.int32)[None, :]
     channel = column % CHANNELS
@@ -39,7 +252,7 @@
     return jnp.stack([first, second], axis=0)
 
 
-def correlate(left, columns):
+def plain_correlate(left, columns):
     return jnp.einsum("pcsi,pcsj->cij", left, columns, preferred_element_type=jnp.float32)
 
 
@@ -49,19 +262,19 @@
     return (jnp.swapaxes(shaped, 0, 1) * scale).astype(jnp.bfloat16)
 
 
-def per_device(voltages):
+def plain_per_device(voltages):
     in_dev = voltages.shape[0]
     spec_dev = voltages.shape[1] // FRAME
     n_ta = lax.axis_size("ta")
     frames = voltages.reshape(in_dev, spec_dev, FRAME)
     earlier = shifted(frames, "ta", 1)
     padded = jnp.concatenate([earlier, frames], axis=1)
-    window = make_window()
+    window = plain_window()
     filtered = jnp.zeros((in_dev, spec_dev, FRAME), jnp.float32)
     for k in range(TAPS):
         filtered = filtered + window[k] * padded[:, k : k + spec_dev, :].astype(jnp.float32)
     filtered = filtered.astype(jnp.bfloat16)
-    table = make_table()
+    table = plain_table()
     spectra = jnp.einsum("isn,nk->ksi", filtered, table, preferred_element_type=jnp.float32).astype(
         jnp.bfloat16
     )
@@ -76,8 +289,93 @@
         tiled=True,
     )
     left = left_operand(own_rows)
-    merged = correlate(left, lax.all_gather(own_rows, "ta", axis=3, tiled=True))
+    merged = plain_correlate(left, lax.all_gather(own_rows, "ta", axis=3, tiled=True))
     return finish(merged, row_count, scale)
+
+
+def pack_kernel(spectra_ref, unread_ref, *out_refs):
+    at = 0
+    for out_ref in out_refs:
+        out_ref[...] = spectra_ref[at : at + out_ref.shape[0]]
+        at += out_ref.shape[0]
+
+
+def pack(spectra, after, sizes):
+    return pl.pallas_call(
+        pack_kernel,
+        in_specs=[
+            pl.BlockSpec(memory_space=pltpu.VMEM),
+            pl.BlockSpec(memory_space=pl.ANY),
+        ],
+        out_shape=[
+            jax.ShapeDtypeStruct((size,) + spectra.shape[1:], spectra.dtype) for size in sizes
+        ],
+        compiler_params=pltpu.CompilerParams(vmem_limit_bytes=60 * 2**20),
+        cost_estimate=pl.CostEstimate(
+            flops=0, bytes_accessed=4 * spectra.size, transcendentals=0
+        ),
+    )(spectra, after)
+
+
+def chunks_of(chan_dev):
+    part = chan_dev // 8
+    sizes = [3 * part, 3 * part, 2 * part]
+    return [(sum(sizes[:at]), size) for at, size in enumerate(sizes)]
+
+
+def per_device(voltages):
+    in_dev = voltages.shape[0]
+    count = voltages.shape[1] // FRAME
+    n_ta, n_aa = lax.axis_size("ta"), lax.axis_size("aa")
+    half = in_dev // 2
+    chan_dev = CHANNELS // n_aa
+    fits = in_dev == 2 * LANES and INPUTS == n_ta * LANES and 2 * count * n_ta * n_aa <= 256
+    if not fits or count < TAPS - 1 or chan_dev % 64:
+        return plain_per_device(voltages)
+    scale = 1.0 / (count * n_ta)
+    me = lax.axis_index("ta")
+    core = lax.rem(me, 2)
+
+    odd = range(1, n_ta, 2)
+    halo_even = lax.ppermute(voltages[:half], "ta", [(d, d + 1) for d in odd if d + 1 < n_ta])
+    halo_odd = lax.ppermute(voltages[half:], "ta", [(d, d + 2) for d in odd if d + 2 < n_ta])
+    keep = lax.dynamic_slice_in_dim(voltages, core * half, half, 0)
+    give = lax.dynamic_slice_in_dim(voltages, (1 - core) * half, half, 0)
+    got = lax.ppermute(give, "ta", [(d, d ^ 1) for d in range(n_ta)])
+
+    window = jnp.asarray(make_window())
+    table = make_table()
+    where = core.astype(jnp.int32).reshape(1)
+
+    def exchange(spectra):
+        moved = lax.all_to_all(spectra, "aa", split_axis=0, concat_axis=0, tiled=True)
+        return moved.transpose(3, 0, 1, 2, 4).reshape(chan_dev, n_aa * 2 * count, half)
+
+    def gather(parts):
+        return lax.all_gather(parts, "ta", axis=0)
+
+    late = exchange(dft(where, [keep, got], ((0, 1), (1, 0)), window, table, n_aa, count))
+    first = gather(late)
+    early = exchange(
+        dft(
+            where,
+            [keep, got, halo_even, halo_odd],
+            ((2, 0), (3, 1)),
+            window,
+            table,
+            n_aa,
+            count,
+            after=[late],
+        )
+    )
+    spread = spread_rows(me // 2, n_ta, n_aa * 2 * count, n_aa)
+    result = None
+    chunks = chunks_of(chan_dev)
+    packed = pack(early, first, [size for _, size in chunks])
+    for (at, size), part in zip(chunks, packed):
+        second = gather(part)
+        result = correlate(where, first, second, spread, result, at, chan_dev, n_aa, scale)
+    return result
 
 
 def solution(mesh):

time: 358 us -> 270 us (0.75)
  Pallas kernels: 0 us -> 93.4 us
  matrix products: 67.3 us -> 0 us
  local copies, waits for them, and re-layouts: 56.4 us -> 12.8 us
  blocking collectives: 64.4 us -> 25.3 us
  waiting for transfers between devices: 146 us -> 115 us
  starting transfers between devices: 4.6 us -> 8.19 us
    pallas_call x0 -> x7, Pallas kernels: none -> 93.4 us  [the longest x3 73.8 us: correlate(): pl.pallas_call(functools.partial(correlate_kernel, scale=scale, groups=n_...]
    all_gather x1 -> x4, waiting for transfers between devices: 112 us -> 33.5 us  [gather(): return lax.all_gather(parts, 'ta', axis=0)]
    dot_general x2 -> x0, matrix products: 67.3 us -> none  [the longest x1 37.5 us: per_device(): jnp.einsum('isn,nk->ksi', filtered, table, preferred_element_type=jnp.flo...]
    ppermute x1 -> x3, waiting for transfers between devices: 34 us -> 79.9 us  [the longest x1 42.2 us: per_device(): lax.ppermute(voltages[half:], 'ta', [(d, d + 2) for d in odd if d + 2 < n...]
    convert_element_type x1 -> x0, local copies, waits for them, and re-layouts: 44.1 us -> none  [finish(): return (jnp.swapaxes(shaped, 0, 1) * scale).astype(jnp.bfloat16)]
    all_to_all x2, blocking collectives: 64.4 us -> 25.3 us  [exchange(): lax.all_to_all(spectra, 'aa', split_axis=0, concat_axis=0, tiled=True)]
    all_to_all x6 -> x0, local copies, waits for them, and re-layouts: 6 us -> none  [the longest x3 3.27 us: per_device(): lax.all_to_all(lax.all_to_all(spectra, 'aa', split_axis=1, concat_axis=3,...]
    slice x4 -> x1, local copies, waits for them, and re-layouts: 0.94 us -> 5.18 us  [per_device(): voltages[half:]]
  transfers between devices with their start and end apart: 2 -> 7, of which waited for: 2 -> 4; matrix products, arithmetic and copies ran while one was open for 1% -> 2% of each run, Pallas kernels for 0% -> 25%
where the time goes in v1:
time: 270 us
  waiting for transfers between devices  115 us (43%)
  Pallas kernels  93.4 us (35%)
  blocking collectives  25.3 us (9%)
  between operations  13.3 us (5%)
  local copies, waits for them, and re-layouts  12.8 us (5%)
  starting transfers between devices  8.19 us (3%)
    pallas_call x3, Pallas kernels, correlate(): pl.pallas_call(functools.partial(correlate_kernel, scale=scale, groups=n_...  73.8 us
    ppermute x1, waiting for transfers between devices, per_device(): lax.ppermute(voltages[half:], 'ta', [(d, d + 2) for d in odd if d + 2 < n...  42.2 us
    ppermute x1, waiting for transfers between devices, per_device(): lax.ppermute(voltages[:half], 'ta', [(d, d + 1) for d in odd if d + 1 < n...  37.8 us
    all_gather x4, waiting for transfers between devices, gather(): return lax.all_gather(parts, 'ta', axis=0)  33.5 us
    all_to_all x2, blocking collectives, exchange(): lax.all_to_all(spectra, 'aa', split_axis=0, concat_axis=0, tiled=True)  25.3 us
    pallas_call x2, Pallas kernels, dft(): pl.pallas_call(functools.partial(dft_kernel, pick=pick, count=count, unre...  11.9 us
    pallas_call x1, Pallas kernels, make_table(): pl.pallas_call(table_kernel, out_shape=jax.ShapeDtypeStruct((2, CHANNELS,...  5.62 us
  transfers between devices with their start and end apart: 7, of which 4 were waited for; matrix products, arithmetic and copies ran while one was open for 2% of the time, Pallas kernels for 25%

profile of v1, /device:TPU:1, one launch (start us, length us, event | category | flops | bytes accessed | tf_op | source)
XLA Modules:
  0.0 269.7 jit_solution(10052199392679285757)
XLA Ops:
  6.5 0.0 all-gather.8.cloned.1.call-start
  6.5 0.0 copy-start.2
  6.5 0.0 copy-start.3
  6.5 5.2 %fusion.27 = (bf16[128,6144]{1,0:T(8,128)(2,1)}, bf16[128,6144]{1,0:T(8,128)(2,1)S(1)}, bf16[128,6144]{1,0:T(8,128)(2,1)S(1)}, bf16[128,6144]{1,0:T(8,128)(2,1)}) fusion(bf16[256,6144]{1,0:T(8,128)(2,1)} %param.4, s32[]{:T(128)S(6)} %select_n.64, s32[]{:T(128)S(6)} %select_n.63), kind=kLoop, calls=%fused_computation.57 | loop fusion | bytes 12582920 | tf_op jit(solution)/shard_map/slice | solution.py:341
  11.7 0.0 copy-start.4
  11.7 0.1 collective-permute-start
  11.8 0.0 copy-done.2
  11.8 0.0 copy-done.3
  11.8 5.6 %shard_map.46.refs_3_.refs_5_ = bf16[2,512,2048]{2,1,0:T(8,128)(2,1)S(1)} custom-call(f32[512,32]{1,0:T(8,128)S(1)} %copy-done.3, f32[512,256]{1,0:T(8,128)S(1)} %copy-done.2), custom_call_target="tpu_custom_call" | custom-call | flops 8388608 | bytes 8388608 | tf_op jit(solution)/shard_map/pallas_call | solution.py:61
  17.5 0.0 copy-start
  17.5 0.0 collective-permute-done.refs_1_
  17.5 0.0 copy-done.4
  17.5 6.0 %shard_map.47 = bf16[4,2,3,128,128]{4,3,2,1,0:T(8,128)(2,1)S(1)} custom-call(s32[1]{0:T(128)} %bitcast.core_ref, bf16[128,6144]{1,0:T(8,128)(2,1)S(1)} %get-tuple-element.13.refs_0_, bf16[128,6144]{1,0:T(8,128)(2,1)S(1)} %collective-permute-done.refs_1_, f32[4,2048]{1,0:T(4,128)S(1)} %copy-done.4, bf16[2,512,2048]{2,1,0:T(8,128)(2,1)S(1)} %shard_map.46.refs_3_.refs_5_), custom_call_target="tpu_custom_call" | custom-call | flops 1610612736 | bytes 7340032 | tf_op jit(solution)/shard_map/pallas_call | solution.py:112
  23.5 0.0 copy-done
  23.5 15.5 %all_to_all.10 = bf16[4,2,3,128,128]{4,3,2,1,0:T(8,128)(2,1)S(1)} all-to-all(bf16[4,2,3,128,128]{4,3,2,1,0:T(8,128)(2,1)S(1)} %shard_map.47), channel_id=1, replica_groups=mesh['aa'=4,'ta'=8] {'aa'}, dimensions={0} | all-to-all | bytes 1572864 | tf_op jit(solution)/shard_map/all_to_all | solution.py:351
  39.0 0.0 copy-start.5
  39.0 0.9 copy-done.5
  39.9 1.4 copy.13
  41.3 0.0 all-gather.8.cloned.1.call-update
  41.3 0.0 all-gather.14.cloned.1.call-start
  41.4 4.7 %collective-permute-start.1 = (bf16[128,6144]{1,0:T(8,128)(2,1)}, bf16[128,6144]{1,0:T(8,128)(2,1)S(1)}, u32[]{:S(2)}, u32[]{:S(2)}) collective-permute-start(bf16[128,6144]{1,0:T(8,128)(2,1)} %get-tuple-element.14), channel_id=1, source_target_pairs={{1,2},{3,4},{5,6},{9,10},{11,12},{13,14},{17,18},{19,20},{21,22},{... | collective-permute-start | bytes 4718600 | tf_op jit(solution)/shard_map/ppermute | solution.py:340
  46.0 3.3 %collective-permute-start.2 = (bf16[128,6144]{1,0:T(8,128)(2,1)}, bf16[128,6144]{1,0:T(8,128)(2,1)S(1)}, u32[]{:S(2)}, u32[]{:S(2)}) collective-permute-start(bf16[128,6144]{1,0:T(8,128)(2,1)} %get-tuple-element.11), channel_id=1, source_target_pairs={{1,3},{3,5},{5,7},{9,11},{11,13},{13,15},{17,19},{19,21},{21,23},{... | collective-permute-start | bytes 4718600 | tf_op jit(solution)/shard_map/ppermute | solution.py:341
  49.3 1.7 copy.14.refs_6_
  51.1 37.8 %collective-permute-done.1.refs_2_ = bf16[128,6144]{1,0:T(8,128)(2,1)S(1)} collective-permute-done((bf16[128,6144]{1,0:T(8,128)(2,1)}, bf16[128,6144]{1,0:T(8,128)(2,1)S(1)}, u32[]{:S(2)}, u32[]{:S(2)}) %collective-permute-start.1) | collective-permute-done | bytes 1572896 | tf_op jit(solution)/shard_map/ppermute | solution.py:340
  88.8 42.2 %collective-permute-done.2.refs_3_ = bf16[128,6144]{1,0:T(8,128)(2,1)S(1)} collective-permute-done((bf16[128,6144]{1,0:T(8,128)(2,1)}, bf16[128,6144]{1,0:T(8,128)(2,1)S(1)}, u32[]{:S(2)}, u32[]{:S(2)}) %collective-permute-start.2) | collective-permute-done | bytes 1572896 | tf_op jit(solution)/shard_map/ppermute | solution.py:341
  131.0 0.0 copy-start.1
  131.0 2.2 copy-done.1
  133.2 5.9 %shard_map.48 = bf16[4,2,3,128,128]{4,3,2,1,0:T(8,128)(2,1)S(1)} custom-call(s32[1]{0:T(128)} %bitcast.core_ref, bf16[128,6144]{1,0:T(8,128)(2,1)S(1)} %get-tuple-element.13.refs_0_, bf16[128,6144]{1,0:T(8,128)(2,1)S(1)} %collective-permute-done.refs_1_, bf16[128,6144]{1,0:T(8,128)(2,1)S(1)} %collective-permute-done.1.refs_2_, ...), custom_call_target="tpu_custom_call" | custom-call | flops 1610612736 | bytes 10485760 | tf_op jit(solution)/shard_map/pallas_call | solution.py:112
  139.1 9.8 %all_to_all.11 = bf16[4,2,3,128,128]{4,3,2,1,0:T(8,128)(2,1)S(1)} all-to-all(bf16[4,2,3,128,128]{4,3,2,1,0:T(8,128)(2,1)S(1)} %shard_map.48), channel_id=1, replica_groups=mesh['aa'=4,'ta'=8] {'aa'}, dimensions={0} | all-to-all | bytes 1572864 | tf_op jit(solution)/shard_map/all_to_all | solution.py:351
  148.9 1.4 copy.15.spectra_ref
  150.3 0.0 all-gather.8.cloned.1.call-done.unread_ref.first_ref
  150.3 2.1 shard_map.49
  152.4 0.0 all-gather.14.cloned.1.call-update
  152.4 0.0 all-gather.12.cloned.1.call-start
  152.5 0.7 all-gather.12.cloned.1.call-update
  153.2 0.0 all-gather.10.cloned.1.call-start
  153.2 0.5 all-gather.10.cloned.1.call-update
  153.9 1.9 select_convert_fusion.spread_ref
  155.8 28.8 %all-gather.14.cloned.1.call-done = bf16[384,24,128]{2,1,0:T(8,128)(2,1)} async-done(((bf16[48,24,128]{2,1,0:T(8,128)(2,1)}), bf16[384,24,128]{2,1,0:T(8,128)(2,1)}) %all-gather.14.cloned.1.call-update) | async-done | bytes 2359312 | tf_op jit(solution)/shard_map/all_gather | solution.py:355
  184.6 27.2 %shard_map.50.refs_0_ = bf16[2,128,128,1024]{3,2,1,0:T(8,128)(2,1)} custom-call(s32[1]{0:T(128)} %bitcast.core_ref, bf16[8,128,24,128]{3,2,1,0:T(8,128)(2,1)} %all-gather.8.cloned.1.call-done.unread_ref.first_ref, bf16[8,48,24,128]{3,2,1,0:T(8,128)(2,1)} %bitcast.15, bf16[256,512]{1,0:T(8,128)(2,1)} %select_convert_fusion.spread_ref), custom_call_target="tpu_custom_call" | custom-call | flops 6442450944 | bytes 29884416 | tf_op jit(solution)/shard_map/pallas_call | solution.py:198
  211.8 4.7 %all-gather.12.cloned.1.call-done = bf16[384,24,128]{2,1,0:T(8,128)(2,1)} async-done(((bf16[48,24,128]{2,1,0:T(8,128)(2,1)}), bf16[384,24,128]{2,1,0:T(8,128)(2,1)}) %all-gather.12.cloned.1.call-update) | async-done | bytes 2359312 | tf_op jit(solution)/shard_map/all_gather | solution.py:355
  216.6 27.3 %shard_map.51.refs_0_ = bf16[2,128,128,1024]{3,2,1,0:T(8,128)(2,1)} custom-call(s32[1]{0:T(128)} %bitcast.core_ref, bf16[8,128,24,128]{3,2,1,0:T(8,128)(2,1)} %all-gather.8.cloned.1.call-done.unread_ref.first_ref, bf16[8,48,24,128]{3,2,1,0:T(8,128)(2,1)} %bitcast.16, bf16[256,512]{1,0:T(8,128)(2,1)} %select_convert_fusion.spread_ref, ...), custom_call_target="tpu_custom_call", output_to_operand_aliasing={{}: (4, {})} | custom-call | flops 6442450944 | bytes 29884416 | tf_op jit(solution)/shard_map/pallas_call | solution.py:198
  243.9 0.0 all-gather.10.cloned.1.call-done
  243.9 19.3 %shard_map.52 = bf16[2,128,128,1024]{3,2,1,0:T(8,128)(2,1)} custom-call(s32[1]{0:T(128)} %bitcast.core_ref, bf16[8,128,24,128]{3,2,1,0:T(8,128)(2,1)} %all-gather.8.cloned.1.call-done.unread_ref.first_ref, bf16[8,32,24,128]{3,2,1,0:T(8,128)(2,1)} %bitcast.17, bf16[256,512]{1,0:T(8,128)(2,1)} %select_convert_fusion.spread_ref, ...), custom_call_target="tpu_custom_call", output_to_operand_aliasing={{}: (4, {})} | custom-call | flops 4294967296 | bytes 19922944 | tf_op jit(solution)/shard_map/pallas_call | solution.py:198
  (8 shorter events, 0.1 us)
Async XLA Ops:
  6.5 143.8 %all-gather.8.cloned.1.call-start = ((), (), s32[]{:S(2)}) async-start(), calls=%async_computation.2 | async-start | bytes 7077888 | tf_op jit(solution)/shard_map/all_gather | solution.py:355
  6.5 5.3 %copy-start.2 = (f32[512,256]{1,0:T(8,128)S(1)}, f32[512,256]{1,0:T(8,128)}, u32[]{:S(2)}) copy-start(f32[512,256]{1,0:T(8,128)} %constant.97.clone.fine_ref) | copy-start | bytes 1572868
  6.5 5.3 %copy-start.3 = (f32[512,32]{1,0:T(8,128)S(1)}, f32[512,32]{1,0:T(8,128)}, u32[]{:S(2)}) copy-start(f32[512,32]{1,0:T(8,128)} %constant.96.clone.coarse_ref) | copy-start | bytes 196612
  11.7 5.8 %copy-start.4 = (f32[4,2048]{1,0:T(4,128)S(1)}, f32[4,2048]{1,0:T(4,128)}, u32[]{:S(2)}) copy-start(f32[4,2048]{1,0:T(4,128)} %constant.95.clone.refs_2_.refs_4_) | copy-start | bytes 98308
  11.7 5.8 %collective-permute-start = (bf16[128,6144]{1,0:T(8,128)(2,1)S(1)}, bf16[128,6144]{1,0:T(8,128)(2,1)S(1)}, u32[]{:S(2)}, u32[]{:S(2)}) collective-permute-start(bf16[128,6144]{1,0:T(8,128)(2,1)S(1)} %get-tuple-element.12), channel_id=1, source_target_pairs={{0,1},{1,0},{2,3},{3,2},{4,5},{5,4},{6,7},{7,6},{8,9},{9,8},{10,11... | collective-permute-start | bytes 4718600 | tf_op jit(solution)/shard_map/ppermute | solution.py:344
  17.5 6.0 %copy-start = (bf16[2,512,2048]{2,1,0:T(8,128)(2,1)}, bf16[2,512,2048]{2,1,0:T(8,128)(2,1)S(1)}, u32[]{:S(2)}) copy-start(bf16[2,512,2048]{2,1,0:T(8,128)(2,1)S(1)} %shard_map.46.refs_3_.refs_5_) | copy-start | bytes 12582916
  39.0 0.9 copy-start.5
  41.3 143.3 %all-gather.14.cloned.1.call-start = ((), (), s32[]{:S(2)}) async-start(), calls=%async_computation.5 | async-start | bytes 2654208 | tf_op jit(solution)/shard_map/all_gather | solution.py:355
  41.4 47.5 %collective-permute-start.1 = (bf16[128,6144]{1,0:T(8,128)(2,1)}, bf16[128,6144]{1,0:T(8,128)(2,1)S(1)}, u32[]{:S(2)}, u32[]{:S(2)}) collective-permute-start(bf16[128,6144]{1,0:T(8,128)(2,1)} %get-tuple-element.14), channel_id=1, source_target_pairs={{1,2},{3,4},{5,6},{9,10},{11,12},{13,14},{17,18},{19,20},{21,22},{... | collective-permute-start | bytes 4718600 | tf_op jit(solution)/shard_map/ppermute | solution.py:340
  46.0 85.0 %collective-permute-start.2 = (bf16[128,6144]{1,0:T(8,128)(2,1)}, bf16[128,6144]{1,0:T(8,128)(2,1)S(1)}, u32[]{:S(2)}, u32[]{:S(2)}) collective-permute-start(bf16[128,6144]{1,0:T(8,128)(2,1)} %get-tuple-element.11), channel_id=1, source_target_pairs={{1,3},{3,5},{5,7},{9,11},{11,13},{13,15},{17,19},{19,21},{21,23},{... | collective-permute-start | bytes 4718600 | tf_op jit(solution)/shard_map/ppermute | solution.py:341
  131.0 2.2 copy-start.1
  152.4 64.1 %all-gather.12.cloned.1.call-start = ((), (), s32[]{:S(2)}) async-start(), calls=%async_computation.4 | async-start | bytes 2654208 | tf_op jit(solution)/shard_map/all_gather | solution.py:355
  153.2 90.7 %all-gather.10.cloned.1.call-start = ((), (), s32[]{:S(2)}) async-start(), calls=%async_computation.3 | async-start | bytes 1769472 | tf_op jit(solution)/shard_map/all_gather | solution.py:355
Sparse Core Ops, SparseCore 0:
  41.4 85.2 all-gather.7
  152.6 32.0 all-gather.13
  186.3 30.2 all-gather.11
  218.1 24.7 all-gather.9

commit v2 on v1

--- a/solution.py
+++ b/solution.py
@@ -134,7 +134,7 @@
 
 
 def correlate_kernel(core_ref, first_ref, second_ref, spread_ref, *refs, scale, groups):
-    out_ref, columns_ref = refs[-2:]
+    out_ref, columns_ref, left_ref = refs[-3:]
     halves, chans, depth, lanes = first_ref.shape
     full = halves * depth
     size = columns_ref.shape[0]
@@ -155,7 +155,6 @@
                     columns_ref[place : place + depth, core * lanes : (core + 1) * lanes] = ref[
                         2 * block + core, c
                     ]
-        columns = columns_ref[...]
         left = lax.dot_general(
             columns_ref[:, own],
             spread_ref[...],
@@ -165,12 +164,16 @@
         for p in range(2):
             part = left[:, p * size : (p + 1) * size]
             for group in range(groups):
-                total = jnp.dot(
-                    part * masks[group], columns, preferred_element_type=jnp.float32
-                )
-                out_ref[p, c, :, group * 2 * lanes : (group + 1) * 2 * lanes] = (
-                    total * scale
-                ).astype(jnp.bfloat16)
+                place = (p * groups + group) * lanes
+                left_ref[place : place + lanes, :] = part * masks[group]
+        total = jnp.dot(left_ref[...], columns_ref[...], preferred_element_type=jnp.float32)
+        value = (total * scale).astype(jnp.bfloat16)
+        for p in range(2):
+            for group in range(groups):
+                place = (p * groups + group) * lanes
+                out_ref[p, c, :, group * 2 * lanes : (group + 1) * 2 * lanes] = value[
+                    place : place + lanes
+                ]
 
 
 def spread_rows(group, halves, depth, groups):
@@ -209,7 +212,10 @@
             out_specs=pl.BlockSpec(
                 (2, step, lanes, INPUTS), lambda c, core_ref: (0, start + c, 0, 0)
             ),
-            scratch_shapes=[pltpu.VMEM((256, 2 * lanes), jnp.bfloat16)],
+            scratch_shapes=[
+                pltpu.VMEM((256, 2 * lanes), jnp.bfloat16),
+                pltpu.VMEM((2 * n_aa * lanes, 256), jnp.bfloat16),
+            ],
         ),
         out_shape=out_shape,
         input_output_aliases={4: 0} if extra else {},
@@ -293,7 +299,8 @@
     return finish(merged, row_count, scale)
 
 
-def pack_kernel(spectra_ref, unread_ref, *out_refs):
+def pack_kernel(spectra_ref, *refs, unread):
+    out_refs = refs[unread:]
     at = 0
     for out_ref in out_refs:
         out_ref[...] = spectra_ref[at : at + out_ref.shape[0]]
@@ -302,11 +309,9 @@
 
 def pack(spectra, after, sizes):
     return pl.pallas_call(
-        pack_kernel,
-        in_specs=[
-            pl.BlockSpec(memory_space=pltpu.VMEM),
-            pl.BlockSpec(memory_space=pl.ANY),
-        ],
+        functools.partial(pack_kernel, unread=len(after)),
+        in_specs=[pl.BlockSpec(memory_space=pltpu.VMEM)]
+        + [pl.BlockSpec(memory_space=pl.ANY)] * len(after),
         out_shape=[
             jax.ShapeDtypeStruct((size,) + spectra.shape[1:], spectra.dtype) for size in sizes
         ],
@@ -314,12 +319,12 @@
         cost_estimate=pl.CostEstimate(
             flops=0, bytes_accessed=4 * spectra.size, transcendentals=0
         ),
-    )(spectra, after)
+    )(spectra, *after)
 
 
 def chunks_of(chan_dev):
     part = chan_dev // 8
-    sizes = [3 * part, 3 * part, 2 * part]
+    sizes = [5 * part, 3 * part]
     return [(sum(sizes[:at]), size) for at, size in enumerate(sizes)]
 
 
@@ -355,6 +360,7 @@
         return lax.all_gather(parts, "ta", axis=0)
 
     late = exchange(dft(where, [keep, got], ((0, 1), (1, 0)), window, table, n_aa, count))
+    (late,) = pack(late, [halo_even, halo_odd], [chan_dev])
     first = gather(late)
     early = exchange(
         dft(
@@ -371,7 +377,7 @@
     spread = spread_rows(me // 2, n_ta, n_aa * 2 * count, n_aa)
     result = None
     chunks = chunks_of(chan_dev)
-    packed = pack(early, first, [size for _, size in chunks])
+    packed = pack(early, [first], [size for _, size in chunks])
     for (at, size), part in zip(chunks, packed):
         second = gather(part)
         result = correlate(where, first, second, spread, result, at, chan_dev, n_aa, scale)

time: 270 us -> 239 us (0.89)
  waiting for transfers between devices: 115 us -> 90 us
  local copies, waits for them, and re-layouts: 12.8 us -> 9.67 us
    all_gather x4 -> x3, waiting for transfers between devices: 33.5 us -> 84.5 us  [gather(): return lax.all_gather(parts, 'ta', axis=0)]
    ppermute x1, waiting for transfers between devices: 42.2 us -> 0.01 us  [per_device(): lax.ppermute(voltages[half:], 'ta', [(d, d + 2) for d in odd if d + 2 < n...]
    ppermute x1, waiting for transfers between devices: 37.8 us -> 4.88 us  [per_device(): lax.ppermute(voltages[:half], 'ta', [(d, d + 1) for d in odd if d + 1 < n...]
    pallas_call x3 -> x2, Pallas kernels: 73.8 us -> 68.2 us  [correlate(): pl.pallas_call(functools.partial(correlate_kernel, scale=scale, groups=n_...]
  transfers between devices with their start and end apart: 7 -> 6, of which waited for: 4 -> 3; matrix products, arithmetic and copies ran while one was open for 2% -> 2% of each run, Pallas kernels for 25% -> 26%
where the time goes in v2:
time: 239 us
  Pallas kernels  91.8 us (38%)
  waiting for transfers between devices  90 us (38%)
  blocking collectives  23.4 us (10%)
  between operations  13.2 us (6%)
  local copies, waits for them, and re-layouts  9.67 us (4%)
  starting transfers between devices  8.73 us (4%)
    all_gather x3, waiting for transfers between devices, gather(): return lax.all_gather(parts, 'ta', axis=0)  84.5 us
    pallas_call x2, Pallas kernels, correlate(): pl.pallas_call(functools.partial(correlate_kernel, scale=scale, groups=n_...  68.2 us
    all_to_all x2, blocking collectives, exchange(): lax.all_to_all(spectra, 'aa', split_axis=0, concat_axis=0, tiled=True)  23.4 us
    pallas_call x2, Pallas kernels, dft(): pl.pallas_call(functools.partial(dft_kernel, pick=pick, count=count, unre...  13.8 us
    ppermute x1, starting transfers between devices, per_device(): lax.ppermute(voltages[half:], 'ta', [(d, d + 2) for d in odd if d + 2 < n...  5.9 us
    pallas_call x1, Pallas kernels, make_table(): pl.pallas_call(table_kernel, out_shape=jax.ShapeDtypeStruct((2, CHANNELS,...  5.62 us
    ppermute x1, waiting for transfers between devices, per_device(): lax.ppermute(voltages[:half], 'ta', [(d, d + 1) for d in odd if d + 1 < n...  4.88 us
  transfers between devices with their start and end apart: 6, of which 3 were waited for; matrix products, arithmetic and copies ran while one was open for 2% of the time, Pallas kernels for 26%

profile of v2, /device:TPU:1, one launch (start us, length us, event | category | flops | bytes accessed | tf_op | source)
XLA Modules:
  0.0 238.9 jit_solution(2708803220072289919)
XLA Ops:
  6.5 0.0 all-gather.7.cloned.1.call-start
  6.5 0.0 copy-start.3
  6.5 0.0 copy-start.4
  6.5 3.5 %fusion.27 = (bf16[128,6144]{1,0:T(8,128)(2,1)S(1)}, bf16[128,6144]{1,0:T(8,128)(2,1)S(1)}, bf16[128,6144]{1,0:T(8,128)(2,1)S(1)}, bf16[128,6144]{1,0:T(8,128)(2,1)S(1)}) fusion(bf16[256,6144]{1,0:T(8,128)(2,1)} %param.4, s32[]{:T(128)S(6)} %select_n.64, s32[]{:T(128)S(6)} %select_n.63), kind=kLoop, calls=%fused_computation.57 | loop fusion | bytes 12582920 | tf_op jit(solution)/shard_map/slice | solution.py:346
  10.1 0.2 collective-permute-start
  10.3 5.9 %collective-permute-start.2 = (bf16[128,6144]{1,0:T(8,128)(2,1)S(1)}, bf16[128,6144]{1,0:T(8,128)(2,1)}, u32[]{:S(2)}, u32[]{:S(2)}) collective-permute-start(bf16[128,6144]{1,0:T(8,128)(2,1)S(1)} %get-tuple-element.9), channel_id=1, source_target_pairs={{1,3},{3,5},{5,7},{9,11},{11,13},{13,15},{17,19},{19,21},{21,23},{... | collective-permute-start | bytes 4718600 | tf_op jit(solution)/shard_map/ppermute | solution.py:346
  16.2 0.0 copy-start.5
  16.2 2.6 %collective-permute-start.1 = (bf16[128,6144]{1,0:T(8,128)(2,1)S(1)}, bf16[128,6144]{1,0:T(8,128)(2,1)}, u32[]{:S(2)}, u32[]{:S(2)}) collective-permute-start(bf16[128,6144]{1,0:T(8,128)(2,1)S(1)} %get-tuple-element.12), channel_id=1, source_target_pairs={{1,2},{3,4},{5,6},{9,10},{11,12},{13,14},{17,18},{19,20},{21,22},{... | collective-permute-start | bytes 4718600 | tf_op jit(solution)/shard_map/ppermute | solution.py:345
  18.7 0.0 copy-done.3
  18.7 0.0 copy-done.4
  18.8 5.6 %shard_map.46.refs_3_.refs_5_ = bf16[2,512,2048]{2,1,0:T(8,128)(2,1)S(1)} custom-call(f32[512,32]{1,0:T(8,128)S(1)} %copy-done.4, f32[512,256]{1,0:T(8,128)S(1)} %copy-done.3), custom_call_target="tpu_custom_call" | custom-call | flops 8388608 | bytes 8388608 | tf_op jit(solution)/shard_map/pallas_call | solution.py:61
  24.4 0.0 copy-start
  24.4 0.0 collective-permute-done.refs_1_
  24.4 0.0 copy-done.5
  24.4 6.0 %shard_map.47 = bf16[4,2,3,128,128]{4,3,2,1,0:T(8,128)(2,1)S(1)} custom-call(s32[1]{0:T(128)} %bitcast.core_ref, bf16[128,6144]{1,0:T(8,128)(2,1)S(1)} %get-tuple-element.11.refs_0_, bf16[128,6144]{1,0:T(8,128)(2,1)S(1)} %collective-permute-done.refs_1_, f32[4,2048]{1,0:T(4,128)S(1)} %copy-done.5, bf16[2,512,2048]{2,1,0:T(8,128)(2,1)S(1)} %shard_map.46.refs_3_.refs_5_), custom_call_target="tpu_custom_call" | custom-call | flops 1610612736 | bytes 7340032 | tf_op jit(solution)/shard_map/pallas_call | solution.py:112
  30.4 0.0 copy-done
  30.4 12.4 %all_to_all.10 = bf16[4,2,3,128,128]{4,3,2,1,0:T(8,128)(2,1)S(1)} all-to-all(bf16[4,2,3,128,128]{4,3,2,1,0:T(8,128)(2,1)S(1)} %shard_map.47), channel_id=1, replica_groups=mesh['aa'=4,'ta'=8] {'aa'}, dimensions={0} | all-to-all | bytes 1572864 | tf_op jit(solution)/shard_map/all_to_all | solution.py:356
  42.8 1.4 copy.10.spectra_ref
  44.2 0.0 collective-permute-done.2.refs_1_.refs_3_
  44.2 4.9 %collective-permute-done.1.refs_0_.refs_2_ = bf16[128,6144]{1,0:T(8,128)(2,1)} collective-permute-done((bf16[128,6144]{1,0:T(8,128)(2,1)S(1)}, bf16[128,6144]{1,0:T(8,128)(2,1)}, u32[]{:S(2)}, u32[]{:S(2)}) %collective-permute-start.1) | collective-permute-done | bytes 1572896 | tf_op jit(solution)/shard_map/ppermute | solution.py:345
  49.1 2.1 shard_map.48.refs_6_
  51.2 0.0 all-gather.7.cloned.1.call-update
  51.2 0.0 all-gather.11.cloned.1.call-start
  51.2 0.0 copy-start.1
  51.3 2.2 copy-done.1
  53.4 0.0 copy-start.2
  53.4 1.1 copy-done.2
  54.6 7.9 %shard_map.49 = bf16[4,2,3,128,128]{4,3,2,1,0:T(8,128)(2,1)S(1)} custom-call(s32[1]{0:T(128)} %bitcast.core_ref, bf16[128,6144]{1,0:T(8,128)(2,1)S(1)} %get-tuple-element.11.refs_0_, bf16[128,6144]{1,0:T(8,128)(2,1)S(1)} %collective-permute-done.refs_1_, bf16[128,6144]{1,0:T(8,128)(2,1)} %collective-permute-done.1.refs_0_.refs_2_, ...), custom_call_target="tpu_custom_call" | custom-call | flops 1610612736 | bytes 10485760 | tf_op jit(solution)/shard_map/pallas_call | solution.py:112
  62.4 11.0 %all_to_all.11 = bf16[4,2,3,128,128]{4,3,2,1,0:T(8,128)(2,1)S(1)} all-to-all(bf16[4,2,3,128,128]{4,3,2,1,0:T(8,128)(2,1)S(1)} %shard_map.49), channel_id=1, replica_groups=mesh['aa'=4,'ta'=8] {'aa'}, dimensions={0} | all-to-all | bytes 1572864 | tf_op jit(solution)/shard_map/all_to_all | solution.py:356
  73.5 1.4 copy.11.spectra_ref
  74.8 43.7 %all-gather.7.cloned.1.call-done = bf16[1024,24,128]{2,1,0:T(8,128)(2,1)} async-done(((bf16[128,24,128]{2,1,0:T(8,128)(2,1)}), bf16[1024,24,128]{2,1,0:T(8,128)(2,1)}) %all-gather.7.cloned.1.call-update) | async-done | bytes 6291472 | tf_op jit(solution)/shard_map/all_gather | solution.py:360
  118.5 2.1 shard_map.50
  120.6 0.0 all-gather.11.cloned.1.call-update
  120.6 0.0 all-gather.9.cloned.1.call-start
  120.7 0.7 all-gather.9.cloned.1.call-update
  121.5 1.9 select_convert_fusion.spread_ref
  123.4 40.8 %all-gather.11.cloned.1.call-done = bf16[640,24,128]{2,1,0:T(8,128)(2,1)} async-done(((bf16[80,24,128]{2,1,0:T(8,128)(2,1)}), bf16[640,24,128]{2,1,0:T(8,128)(2,1)}) %all-gather.11.cloned.1.call-update) | async-done | bytes 3932176 | tf_op jit(solution)/shard_map/all_gather | solution.py:360
  164.2 41.8 %shard_map.51.refs_0_ = bf16[2,128,128,1024]{3,2,1,0:T(8,128)(2,1)} custom-call(s32[1]{0:T(128)} %bitcast.core_ref, bf16[8,128,24,128]{3,2,1,0:T(8,128)(2,1)} %bitcast.11, bf16[8,80,24,128]{3,2,1,0:T(8,128)(2,1)} %bitcast.13, bf16[256,512]{1,0:T(8,128)(2,1)} %select_convert_fusion.spread_ref), custom_call_target="tpu_custom_call" | custom-call | flops 10737418240 | bytes 49807360 | tf_op jit(solution)/shard_map/pallas_call | solution.py:201
  206.0 0.0 all-gather.9.cloned.1.call-done
  206.0 26.4 %shard_map.52 = bf16[2,128,128,1024]{3,2,1,0:T(8,128)(2,1)} custom-call(s32[1]{0:T(128)} %bitcast.core_ref, bf16[8,128,24,128]{3,2,1,0:T(8,128)(2,1)} %bitcast.12, bf16[8,48,24,128]{3,2,1,0:T(8,128)(2,1)} %bitcast.16, bf16[256,512]{1,0:T(8,128)(2,1)} %select_convert_fusion.spread_ref, ...), custom_call_target="tpu_custom_call", output_to_operand_aliasing={{}: (4, {})} | custom-call | flops 6442450944 | bytes 29884416 | tf_op jit(solution)/shard_map/pallas_call | solution.py:201
  (8 shorter events, 0.1 us)
Async XLA Ops:
  6.5 112.0 %all-gather.7.cloned.1.call-start = ((), (), s32[]{:S(2)}) async-start(), calls=%async_computation.2 | async-start | bytes 7077888 | tf_op jit(solution)/shard_map/all_gather | solution.py:360
  6.5 12.2 %copy-start.3 = (f32[512,256]{1,0:T(8,128)S(1)}, f32[512,256]{1,0:T(8,128)}, u32[]{:S(2)}) copy-start(f32[512,256]{1,0:T(8,128)} %constant.97.clone.fine_ref) | copy-start | bytes 1572868
  6.5 12.2 %copy-start.4 = (f32[512,32]{1,0:T(8,128)S(1)}, f32[512,32]{1,0:T(8,128)}, u32[]{:S(2)}) copy-start(f32[512,32]{1,0:T(8,128)} %constant.96.clone.coarse_ref) | copy-start | bytes 196612
  10.1 14.3 %collective-permute-start = (bf16[128,6144]{1,0:T(8,128)(2,1)S(1)}, bf16[128,6144]{1,0:T(8,128)(2,1)S(1)}, u32[]{:S(2)}, u32[]{:S(2)}) collective-permute-start(bf16[128,6144]{1,0:T(8,128)(2,1)S(1)} %get-tuple-element.10), channel_id=1, source_target_pairs={{0,1},{1,0},{2,3},{3,2},{4,5},{5,4},{6,7},{7,6},{8,9},{9,8},{10,11... | collective-permute-start | bytes 4718600 | tf_op jit(solution)/shard_map/ppermute | solution.py:349
  10.3 34.0 %collective-permute-start.2 = (bf16[128,6144]{1,0:T(8,128)(2,1)S(1)}, bf16[128,6144]{1,0:T(8,128)(2,1)}, u32[]{:S(2)}, u32[]{:S(2)}) collective-permute-start(bf16[128,6144]{1,0:T(8,128)(2,1)S(1)} %get-tuple-element.9), channel_id=1, source_target_pairs={{1,3},{3,5},{5,7},{9,11},{11,13},{13,15},{17,19},{19,21},{21,23},{... | collective-permute-start | bytes 4718600 | tf_op jit(solution)/shard_map/ppermute | solution.py:346
  16.2 8.2 %copy-start.5 = (f32[4,2048]{1,0:T(4,128)S(1)}, f32[4,2048]{1,0:T(4,128)}, u32[]{:S(2)}) copy-start(f32[4,2048]{1,0:T(4,128)} %constant.95.clone.refs_2_.refs_4_) | copy-start | bytes 98308
  16.2 32.9 %collective-permute-start.1 = (bf16[128,6144]{1,0:T(8,128)(2,1)S(1)}, bf16[128,6144]{1,0:T(8,128)(2,1)}, u32[]{:S(2)}, u32[]{:S(2)}) collective-permute-start(bf16[128,6144]{1,0:T(8,128)(2,1)S(1)} %get-tuple-element.12), channel_id=1, source_target_pairs={{1,2},{3,4},{5,6},{9,10},{11,12},{13,14},{17,18},{19,20},{21,22},{... | collective-permute-start | bytes 4718600 | tf_op jit(solution)/shard_map/ppermute | solution.py:345
  24.4 6.0 %copy-start = (bf16[2,512,2048]{2,1,0:T(8,128)(2,1)}, bf16[2,512,2048]{2,1,0:T(8,128)(2,1)S(1)}, u32[]{:S(2)}) copy-start(bf16[2,512,2048]{2,1,0:T(8,128)(2,1)S(1)} %shard_map.46.refs_3_.refs_5_) | copy-start | bytes 12582916
  51.2 113.0 %all-gather.11.cloned.1.call-start = ((), (), s32[]{:S(2)}) async-start(), calls=%async_computation.4 | async-start | bytes 4423680 | tf_op jit(solution)/shard_map/all_gather | solution.py:360
  51.2 2.2 copy-start.1
  53.4 1.1 copy-start.2
  120.6 85.3 %all-gather.9.cloned.1.call-start = ((), (), s32[]{:S(2)}) async-start(), calls=%async_computation.3 | async-start | bytes 2654208 | tf_op jit(solution)/shard_map/all_gather | solution.py:360
Sparse Core Ops, SparseCore 0:
  51.3 67.1 all-gather.6
  120.8 43.4 all-gather.10
  165.9 30.3 all-gather.8
